TPU v7x, 256 devices: a whole 4x4x8 slice. The times are simulated.
256 devices in a mesh: seq: 32 (over z_hi, x, core), exp: 8 (over z_lo, y).
Axes of the slice: x: 4, y: 4, z: 8 (z_hi: 4, z_lo: 2; z = z_hi * 2 + z_lo), core: 2. Of those that a mesh axis runs over, the one named last changes fastest.
Arguments:
- tokens: bfloat16 [4096, 2304], P('seq'), may hold values from -6 to 6
- norm_gain: bfloat16 [2304], replicated, may hold values from 0.099609375 to 1.8984375
- w_qkv: bfloat16 [2304, 3, 2048], P(None, None, 'exp'), may hold values from -12 to 12
- w_out: bfloat16 [2048, 2304], P('exp'), may hold values from -0.125 to 0.125
- moe_gain: bfloat16 [2304], replicated, may hold values from 0.099609375 to 1.8984375
- w_router: bfloat16 [2304, 8], replicated, may hold values from -0.25 to 0.25
- gate_up: bfloat16 [8, 2, 2304, 5760], P('exp', None, None, 'seq'), may hold values from -0.125 to 0.125
- w_down: bfloat16 [8, 5760, 2304], P('exp', 'seq'), may hold values from -0.078125 to 0.078125
- lengths: int32 [4], replicated, may hold values from 1 to 3072, as said below
- blocks_seen: int32 [32, 32], P('seq'), may hold values from 0 to 1, as said below
- expert_ids: int32 [4096, 2], P(('seq', 'exp')), may hold values from 0 to 7, all different within a row; in each aligned block of 16 rows (0 to 15, 16 to 31, ...) at most 8 rows name the same one
- old_place: int32 [8], replicated, may hold values from 0 to 7, each once
- new_place: int32 [8], replicated, may hold values from 0 to 7, each once
Outputs:
- layer_out: bfloat16 [4096, 2304], P(('seq', 'exp'))
- new_gate_up: bfloat16 [8, 2, 2304, 5760], P('exp', None, None, 'seq')
- new_down: bfloat16 [8, 5760, 2304], P('exp', 'seq')
Inputs may be any that keep to these rules, and one draw needn't show every extreme that they name: `lengths`: positive, summing to 4096, the largest exactly 3072. `blocks_seen`: 1 on the diagonal; 0 above it and wherever no sequence has tokens in both blocks; elsewhere 0 or 1. `expert_ids`: the two experts of a token differ; among the 16 tokens of one device no expert is named more than 8 times, and in some devices one expert exactly 8 times. `old_place`: a permutation of the experts. `new_place`: a permutation of the experts.
All inputs are finite; a program needn't handle non-finite values.
Results may differ from a plain program's by a relative error of at most 0.023.
Values may be sent and summed in bfloat16 or wider, within the bound.
No kernel may reach another device: no remote copies, remote signals or barrier semaphores. Data moves between devices by JAX's collectives and lax.ppermute only.
A program may use at most 128 MiB of HBM per device.

v0:
```python
import jax
import jax.numpy as jnp
from jax import lax
from jax.sharding import PartitionSpec as P

HEAD_DIM = 64
epsilon = 1e-05
masked_score = -1e30


def rms_scale(values_in, gain):
    widened = values_in.astype(jnp.float32)
    inverse = lax.rsqrt(jnp.mean(widened * widened, axis=-1, keepdims=True) + epsilon)
    return widened * inverse * gain.astype(jnp.float32)


def rotate(vectors, angle_base):
    halfway = vectors.shape[-1] // 2
    spacing = jnp.arange(halfway, dtype=jnp.float32) / halfway
    freqs_all = jnp.exp(-jnp.log(10000.0) * spacing)
    angles = angle_base[:, None] * freqs_all[None, :]
    cosine = jnp.cos(angles)[:, None, :]
    sine_part = jnp.sin(angles)[:, None, :]
    leading = vectors[..., :halfway]
    trailing = vectors[..., halfway:]
    return jnp.concatenate(
        [leading * cosine - trailing * sine_part, trailing * cosine + leading * sine_part], axis=-1
    )


def doc_layout(seq_lengths, row_ids):
    ending = jnp.cumsum(seq_lengths, dtype=jnp.int32)
    passed = (ending[None, :] <= row_ids[:, None]).astype(jnp.int32)
    doc_ids = jnp.sum(passed, axis=1, dtype=jnp.int32)
    starting = jnp.sum(passed * seq_lengths[None, :], axis=1, dtype=jnp.int32)
    return (doc_ids, row_ids - starting)


def owner_table(placing):
    slot_range = jnp.arange(placing.shape[0], dtype=jnp.int32)
    return jnp.sum(
        jnp.where(placing[:, None] == slot_range[None, :], slot_range[:, None], 0),
        axis=0,
        dtype=jnp.int32,
    )


def attend_block(
    carried,
    queries,
    query_rows,
    query_docs,
    key_block,
    value_block,
    key_rows,
    seq_lengths,
    seen_row,
    block_rows,
):
    key_docs, _ = doc_layout(seq_lengths, key_rows)
    key_blocks = jnp.floor_divide(key_rows, block_rows)
    block_range = jnp.arange(seen_row.shape[0], dtype=jnp.int32)
    key_seen = (
        jnp.sum(
            jnp.where(key_blocks[:, None] == block_range[None, :], seen_row[None, :], 0),
            axis=1,
            dtype=jnp.int32,
        )
        > 0
    )
    allowed = (
        (query_docs[:, None] == key_docs[None, :])
        & (key_rows[None, :] <= query_rows[:, None])
        & key_seen[None, :]
    )
    score_scale = queries.shape[-1] ** (-0.5)

    def compute(state_in):
        largest, totals, summed = state_in
        scores = (
            jnp.einsum("qhd,khd->hqk", queries, key_block, preferred_element_type=jnp.float32)
            * score_scale
        )
        scores = jnp.where(allowed[None], scores, masked_score)
        new_largest = jnp.maximum(largest, jnp.max(scores, axis=2))
        weights = jnp.where(allowed[None], jnp.exp(scores - new_largest[:, :, None]), 0.0)
        totals = jnp.sum(weights, axis=2)
        summed = jnp.einsum(
            "hqk,khd->hqd",
            weights.astype(jnp.bfloat16),
            value_block,
            preferred_element_type=jnp.float32,
        )
        return (new_largest, totals, summed)

    def unchanged(state_in):
        return state_in

    return lax.cond(jnp.any(allowed), compute, unchanged, carried)


def shards(
    tokens,
    norm_gain,
    w_qkv,
    w_out,
    moe_gain,
    w_router,
    gate_up,
    w_down,
    lengths,
    blocks_seen,
    expert_ids,
    old_place,
    new_place,
):
    block_rows = tokens.shape[0]
    model_width = tokens.shape[1]
    exp_count = lax.axis_size("exp")
    block_index = lax.axis_index("seq")
    slot_index = lax.axis_index("exp")
    heads_here = w_qkv.shape[2] // HEAD_DIM
    query_rows = block_index * block_rows + jnp.arange(block_rows, dtype=jnp.int32)
    query_docs, query_places = doc_layout(lengths, query_rows)
    normed = rms_scale(tokens, norm_gain).astype(jnp.bfloat16)
    projected = jnp.dot(
        normed,
        w_qkv.reshape(model_width, 3 * heads_here * HEAD_DIM),
        preferred_element_type=jnp.float32,
    )
    projected = projected.reshape(block_rows, 3, heads_here, HEAD_DIM)
    angle_rows = query_places.astype(jnp.float32)
    queries = rotate(projected[:, 0], angle_rows).astype(jnp.bfloat16)
    key_block = rotate(projected[:, 1], angle_rows).astype(jnp.bfloat16)
    value_block = projected[:, 2].astype(jnp.bfloat16)
    seen_row = blocks_seen[0]
    initial = (
        jnp.full((heads_here, block_rows), masked_score, jnp.float32),
        jnp.zeros((heads_here, block_rows), jnp.float32),
        jnp.zeros((heads_here, block_rows, HEAD_DIM), jnp.float32),
    )
    pieces = (
        lax.all_gather(key_block, "seq", axis=0, tiled=True),
        lax.all_gather(value_block, "seq", axis=0, tiled=True),
    )
    key_rows = jnp.arange(pieces[0].shape[0], dtype=jnp.int32)
    largest, totals, summed = attend_block(
        initial,
        queries,
        query_rows,
        query_docs,
        pieces[0],
        pieces[1],
        key_rows,
        lengths,
        seen_row,
        block_rows,
    )
    attended = (summed / totals[:, :, None]).astype(jnp.bfloat16)
    attended = jnp.transpose(attended, (1, 0, 2)).reshape(block_rows, heads_here * HEAD_DIM)
    shard_rows = block_rows // exp_count
    rows_in = attended
    head_total = lax.psum_scatter(
        jnp.dot(rows_in, w_out, preferred_element_type=jnp.float32).astype(jnp.bfloat16),
        "exp",
        scatter_dimension=0,
        tiled=True,
    ).astype(jnp.float32)
    residual = lax.dynamic_slice_in_dim(tokens, slot_index * shard_rows, shard_rows, 0)
    hidden = (residual.astype(jnp.float32) + head_total).astype(jnp.bfloat16)
    moe_in = rms_scale(hidden, moe_gain).astype(jnp.bfloat16)
    logits = jnp.dot(moe_in, w_router, preferred_element_type=jnp.float32)
    expert_count = w_router.shape[1]
    expert_range = jnp.arange(expert_count, dtype=jnp.int32)
    chosen = jnp.sum(
        jnp.where(expert_ids[:, :, None] == expert_range[None, None, :], logits[:, None, :], 0.0),
        axis=2,
    )
    gate_first = 1.0 / (1.0 + jnp.exp(chosen[:, 1] - chosen[:, 0]))
    gate_second = 1.0 / (1.0 + jnp.exp(chosen[:, 0] - chosen[:, 1]))
    gating = jnp.stack([gate_first, gate_second], axis=1)
    slot_old = owner_table(old_place)
    source_slot = jnp.sum(
        jnp.where(new_place[:, None] == expert_range[None, :], slot_old[None, :], 0),
        axis=1,
        dtype=jnp.int32,
    )
    slice_width = gate_up.shape[3]
    piece_width = model_width // exp_count
    gate_split = gate_up.reshape(2, exp_count, piece_width, slice_width)
    down_split = w_down.reshape(slice_width, exp_count, piece_width)
    gate_held, down_held = (
        lax.all_to_all(gate_split, "exp", split_axis=1, concat_axis=1, tiled=True),
        lax.all_to_all(down_split, "exp", split_axis=1, concat_axis=1, tiled=True),
    )
    gate_sorted = jnp.take(gate_held, source_slot, axis=1)
    down_sorted = jnp.take(down_held, source_slot, axis=1)
    gate_moved, down_moved = (
        lax.all_to_all(gate_sorted, "exp", split_axis=1, concat_axis=1, tiled=True),
        lax.all_to_all(down_sorted, "exp", split_axis=1, concat_axis=1, tiled=True),
    )
    new_gate_up = gate_moved.reshape(1, 2, model_width, slice_width)
    new_down = down_moved.reshape(1, slice_width, model_width)
    owners = owner_table(new_place)
    column_gate = new_gate_up[0]
    column_down = new_down[0]
    capacity = min(shard_rows, 4 * shard_rows // exp_count)
    slot_total = exp_count * capacity
    pair_ids = expert_ids.reshape(-1)
    pair_marks = (pair_ids[:, None] == expert_range[None, :]).astype(jnp.int32)
    earlier = jnp.cumsum(pair_marks, axis=0, dtype=jnp.int32) - pair_marks
    rank_in = jnp.sum(earlier * pair_marks, axis=1, dtype=jnp.int32)
    owner_of = jnp.sum(pair_marks * owners[None, :], axis=1, dtype=jnp.int32)
    target = owner_of * capacity + rank_in
    selector = target[:, None] == jnp.arange(slot_total, dtype=jnp.int32)[None, :]
    repeated = jnp.repeat(moe_in, 2, axis=0)
    outgoing = jnp.einsum(
        "as,ad->sd", selector.astype(jnp.bfloat16), repeated, preferred_element_type=jnp.float32
    )
    outgoing = outgoing.astype(jnp.bfloat16).reshape(exp_count, capacity, model_width)
    arrived = lax.all_to_all(outgoing, "exp", split_axis=0, concat_axis=0, tiled=True)
    source_count = arrived.shape[0]
    item_count = arrived.shape[1]
    pieces = lax.all_gather(arrived, "seq", axis=0, tiled=True)
    flat_rows = pieces.reshape(-1, model_width)
    projected_pair = jnp.einsum(
        "rd,cdf->crf", flat_rows, column_gate, preferred_element_type=jnp.float32
    )
    activated = (jax.nn.silu(projected_pair[0]) * projected_pair[1]).astype(jnp.bfloat16)
    hidden_all = activated.reshape(pieces.shape[0], item_count, slice_width)
    rows_in = hidden_all
    flat_out = jnp.dot(
        rows_in.reshape(-1, slice_width), column_down, preferred_element_type=jnp.float32
    )
    column_sum = lax.psum_scatter(
        flat_out.reshape(source_count * lax.axis_size("seq"), item_count, model_width).astype(
            jnp.bfloat16
        ),
        "seq",
        scatter_dimension=0,
        tiled=True,
    )
    returned = lax.all_to_all(column_sum, "exp", split_axis=0, concat_axis=0, tiled=True)
    pair_gates = gating.reshape(-1)
    spread = jnp.sum(
        jnp.where(selector, pair_gates[:, None], 0.0).reshape(shard_rows, 2, slot_total), axis=1
    )
    moe_sum = jnp.dot(
        spread,
        returned.reshape(slot_total, model_width).astype(jnp.float32),
        precision=lax.Precision.HIGHEST,
    )
    layer_out = (hidden.astype(jnp.float32) + moe_sum).astype(jnp.bfloat16)
    return (layer_out, new_gate_up, new_down)


def solution(mesh):
    in_specs = (
        P("seq", None),
        P(),
        P(None, None, "exp"),
        P("exp", None),
        P(),
        P(),
        P("exp", None, None, "seq"),
        P("exp", "seq", None),
        P(),
        P("seq", None),
        P(("seq", "exp"), None),
        P(),
        P(),
    )
    out_specs = (P(("seq", "exp"), None), P("exp", None, None, "seq"), P("exp", "seq", None))
    return jax.shard_map(shards, mesh=mesh, in_specs=in_specs, out_specs=out_specs, check_vma=False)
```

profile of v0, /device:TPU:8, one launch (start us, length us, event | category | flops | bytes accessed | tf_op | source)
XLA Modules:
  0.0 512.6 jit_solution(13582045412710372037)
XLA Ops:
  10.9 5.9 %copy.61 = bf16[2304,3,256]{0,2,1:T(8,128)(2,1)} copy(bf16[2304,3,256]{2,0,1:T(8,128)(2,1)} %param.17) | data formatting | bytes 7077888 | tf_op args[2]
  16.8 3.2 fusion.25
  24.2 55.6 %all-gather.5.cloned.1.call-done = bf16[4096,4,64]{0,2,1:T(8,128)(2,1)} async-done(((bf16[128,4,64]{0,2,1:T(8,128)(2,1)}), bf16[4096,4,64]{0,2,1:T(8,128)(2,1)}) %all-gather.5.cloned.1.call-update) | async-done | bytes 2097168 | tf_op jit(solution)/shard_map/all_gather | solution.py:143
  79.8 56.4 %all-gather.9.cloned.1.call-done = bf16[4096,1,4,64]{0,3,2,1:T(8,128)(2,1)} async-done(((bf16[128,1,4,64]{0,3,2,1:T(8,128)(2,1)}), bf16[4096,1,4,64]{0,3,2,1:T(8,128)(2,1)}) %all-gather.9.cloned.1.call-update) | async-done | bytes 2097168 | tf_op jit(solution)/shard_map/all_gather | solution.py:144
  136.2 8.4 %conditional.1 = (f32[4,128]{1,0:T(4,128)S(1)}, f32[4,128,64]{1,2,0:T(8,128)S(1)}) conditional(s32[]{:T(128)} %convert_element_type.83, () %tuple.16, (pred[128,4096]{1,0:T(8,128)(4,1)S(1)}, bf16[128,4,64]{0,2,1:T(8,128)(2,1)S(1)}, bf16[4096,4,64]{0,2,1:T(8,128)(2,1)}, bf16[4096,4,64]{0,2,1:T(8,128)(2,1)}) %tuple.47), branch_computations={%region_7.8_spmd, %region_8.11_spmd} | conditional | flops 564133376 | bytes 39530540 | solution.py:99
  136.2 3.6 fusion
  139.8 2.3 fusion.3
  142.1 2.5 fusion.2
  146.8 34.4 %reduce-scatter.5.cloned.1.call-done = bf16[16,2304]{1,0:T(8,128)(2,1)} async-done(((bf16[128,2304]{1,0:T(8,128)(2,1)}), bf16[16,2304]{1,0:T(8,128)(2,1)}) %reduce-scatter.5.cloned.1.call-update) | async-done | bytes 73744 | tf_op jit(solution)/shard_map/reduce_scatter | solution.py:163
  182.8 12.7 %all_to_all.30 = bf16[8,8,2304]{2,1,0:T(8,128)(2,1)} all-to-all(bf16[8,8,2304]{2,1,0:T(8,128)(2,1)S(1)} %fusion.11), channel_id=1, replica_groups=mesh['seq'=32,'exp'=8] {'exp'}, dimensions={0} | all-to-all | bytes 589824 | tf_op jit(solution)/shard_map/all_to_all | solution.py:221
  198.4 4.9 all-to-all-start.3
  203.3 5.4 %reshape.255 = bf16[2,8,288,180]{2,1,0,3:T(8,128)(2,1)S(1)} reshape(bf16[1,2,2304,180]{2,1,3,0:T(2,128)(2,1)} %param.21) | data formatting | bytes 3317760 | tf_op jit(solution)/shard_map/reshape | solution.py:190
  208.7 3.1 copy.65
  211.7 8.9 %all-to-all-done.3 = bf16[180,8,288]{2,0,1:T(8,128)(2,1)S(1)} async-done(((bf16[180,8,288]{2,0,1:T(8,128)(2,1)}), bf16[180,8,288]{2,0,1:T(8,128)(2,1)S(1)}, u32[]{:S(2)}, u32[]{:S(2)}) %all-to-all-start.3) | async-done | bytes 829472 | tf_op jit(solution)/shard_map/all_to_all | solution.py:194
  220.6 4.6 all-to-all-start
  227.0 2.4 select_bitcast_fusion
  229.5 52.2 %all-to-all-done = bf16[2,8,288,180]{2,0,3,1:T(2,128)(2,1)S(1)} async-done(((bf16[2,8,288,180]{2,0,3,1:T(2,128)(2,1)}), bf16[2,8,288,180]{2,0,3,1:T(2,128)(2,1)S(1)}, u32[]{:S(2)}, u32[]{:S(2)}) %all-to-all-start) | async-done | bytes 1658912 | tf_op jit(solution)/shard_map/all_to_all | solution.py:193
  281.7 6.3 %all-to-all-start.4 = ((bf16[180,8,288]{2,0,1:T(8,128)(2,1)}), bf16[180,8,288]{2,0,1:T(8,128)(2,1)S(1)}, u32[]{:S(2)}, u32[]{:S(2)}) async-start(bf16[180,8,288]{2,0,1:T(8,128)(2,1)} %select_bitcast_fusion), calls=%async_computation.5 | async-start | bytes 2260992 | tf_op jit(solution)/shard_map/all_to_all | solution.py:200
  288.0 6.3 %gather_fusion = bf16[8,2,288,180]{2,1,3,0:T(2,128)(2,1)} fusion(bf16[2,8,288,180]{2,0,3,1:T(2,128)(2,1)S(1)} %all-to-all-done, s32[1024]{0:T(1024)S(1)} %pad_clamp_fusion), kind=kCustom, calls=%fused_computation | custom fusion | bytes 3317792 | tf_op jit(solution)/shard_map/jit(_take)/gather | solution.py:196
  294.4 4.9 fusion.16
  299.3 6.4 %all-to-all-done.4 = bf16[180,8,288]{2,0,1:T(8,128)(2,1)S(1)} async-done(((bf16[180,8,288]{2,0,1:T(8,128)(2,1)}), bf16[180,8,288]{2,0,1:T(8,128)(2,1)S(1)}, u32[]{:S(2)}, u32[]{:S(2)}) %all-to-all-start.4) | async-done | bytes 829472 | tf_op jit(solution)/shard_map/all_to_all | solution.py:200
  306.7 6.2 %all-to-all-start.1 = ((bf16[2,8,288,180]{2,0,3,1:T(2,128)(2,1)}), bf16[2,8,288,180]{2,0,3,1:T(2,128)(2,1)S(1)}, u32[]{:S(2)}, u32[]{:S(2)}) async-start(bf16[2,8,288,180]{2,0,3,1:T(2,128)(2,1)} %fusion.16), calls=%async_computation.2 | async-start | bytes 4423680 | tf_op jit(solution)/shard_map/all_to_all | solution.py:199
  316.1 12.4 %all-to-all-done.1 = bf16[2,8,288,180]{2,0,3,1:T(2,128)(2,1)S(1)} async-done(((bf16[2,8,288,180]{2,0,3,1:T(2,128)(2,1)}), bf16[2,8,288,180]{2,0,3,1:T(2,128)(2,1)S(1)}, u32[]{:S(2)}, u32[]{:S(2)}) %all-to-all-start.1) | async-done | bytes 1658912 | tf_op jit(solution)/shard_map/all_to_all | solution.py:199
  330.2 4.2 squeeze_reshape.6
  334.4 6.8 %fusion.13 = f32[2,2048,180]{1,2,0:T(8,128)S(1)} fusion(bf16[2,2304,180]{1,2,0:T(8,128)(2,1)} %squeeze_reshape.6, bf16[256,8,2304]{2,1,0:T(8,128)(2,1)} %all-gather.7.cloned.1.call-done), kind=kOutput, calls=%fused_computation.22 | convolution fusion | flops 3397386240 | bytes 14045184 | tf_op jit(solution)/shard_map/rd,cdf->crf/dot_general | solution.py:226
  342.5 2.2 copy.67
  344.7 7.8 %convert_bitcast_fusion = bf16[8,32,8,2304]{3,2,1,0:T(8,128)(2,1)} fusion(bf16[180,2304,1]{1,0,2:T(8,128)(2,1)} %reshape.254, bf16[256,8,180]{2,1,0:T(8,128)(2,1)} %bitcast.73), kind=kOutput, calls=%fused_computation.15 | convolution fusion | flops 1703411712 | bytes 11003904 | tf_op jit(solution)/shard_map/dot_general | solution.py:232
  352.6 8.5 %copy.82 = bf16[8,32,8,2304]{3,2,0,1:T(8,128)(2,1)} copy(bf16[8,32,8,2304]{3,2,1,0:T(8,128)(2,1)} %convert_bitcast_fusion) | data formatting | bytes 18874368
  361.2 1.9 reshape.234
  363.2 126.2 %reduce-scatter.7.cloned.1.call-done = bf16[8,18432]{1,0:T(8,128)(2,1)} async-done(((bf16[256,18432]{1,0:T(8,128)(2,1)}), bf16[8,18432]{1,0:T(8,128)(2,1)}) %reduce-scatter.7.cloned.1.call-update) | async-done | bytes 294928
  491.1 4.9 all-to-all-start.5
  498.0 6.3 %reshape.257 = bf16[1,2,2304,180]{2,1,3,0:T(2,128)(2,1)} reshape(bf16[2,8,288,180]{2,1,0,3:T(8,128)(2,1)} %copy.78) | data formatting | bytes 3317760
  (93 shorter events, 28.5 us)
Async XLA Ops:
  7.2 137.5 %copy-start = (bf16[256,2304]{1,0:T(8,128)(2,1)S(1)}, bf16[256,2304]{1,0:T(8,128)(2,1)}, u32[]{:S(2)}) copy-start(bf16[256,2304]{1,0:T(8,128)(2,1)} %param.18) | copy-start | bytes 3538948
  7.2 72.6 %all-gather.5.cloned.1.call-start = ((), (), s32[]{:S(2)}) async-start(), calls=%async_computation.8 | async-start | bytes 2162688 | tf_op jit(solution)/shard_map/all_gather | solution.py:143
  10.9 5.9 %copy-start.3 = (bf16[128,2304]{1,0:T(8,128)(2,1)S(1)}, bf16[128,2304]{1,0:T(8,128)(2,1)}, u32[]{:S(2)}) copy-start(bf16[128,2304]{1,0:T(8,128)(2,1)} %param.15) | copy-start | bytes 1769476
  16.8 5.0 copy-start.8
  20.8 115.4 %all-gather.9.cloned.1.call-start = ((), (), s32[]{:S(2)}) async-start(), calls=%async_computation.11 | async-start | bytes 2162688 | tf_op jit(solution)/shard_map/all_gather | solution.py:144
  21.6 159.6 %reduce-scatter.5.cloned.1.call-start = ((), (), s32[]{:S(2)}) async-start(), calls=%async_computation.9 | async-start | bytes 663552 | tf_op jit(solution)/shard_map/reduce_scatter | solution.py:163
  136.2 3.6 copy-start.10
  144.6 1.3 copy-start.7
  144.6 1.5 copy-start.6
  144.6 1.7 copy-start.11
  144.7 1.7 copy-start.9
  144.7 50.8 %copy-start.4 = (bf16[1,180,2304]{2,1,0:T(8,128)(2,1)S(1)}, bf16[1,180,2304]{2,1,0:T(8,128)(2,1)}, u32[]{:S(2)}) copy-start(bf16[1,180,2304]{2,1,0:T(8,128)(2,1)} %param.22) | copy-start | bytes 2488324
  145.9 188.5 %all-gather.7.cloned.1.call-start = ((), (), s32[]{:S(2)}) async-start(), calls=%async_computation.10 | async-start | bytes 9732096 | tf_op jit(solution)/shard_map/all_gather | solution.py:224
  198.4 22.3 %all-to-all-start.3 = ((bf16[180,8,288]{2,0,1:T(8,128)(2,1)}), bf16[180,8,288]{2,0,1:T(8,128)(2,1)S(1)}, u32[]{:S(2)}, u32[]{:S(2)}) async-start(bf16[180,8,288]{2,0,1:T(8,128)(2,1)} %copy.68), calls=%async_computation.4 | async-start | bytes 2260992 | tf_op jit(solution)/shard_map/all_to_all | solution.py:194
  220.6 61.0 %all-to-all-start = ((bf16[2,8,288,180]{2,0,3,1:T(2,128)(2,1)}), bf16[2,8,288,180]{2,0,3,1:T(2,128)(2,1)S(1)}, u32[]{:S(2)}, u32[]{:S(2)}) async-start(bf16[2,8,288,180]{2,0,3,1:T(2,128)(2,1)} %copy.65), calls=%async_computation.1 | async-start | bytes 4423680 | tf_op jit(solution)/shard_map/all_to_all | solution.py:193
  281.7 24.0 %all-to-all-start.4 = ((bf16[180,8,288]{2,0,1:T(8,128)(2,1)}), bf16[180,8,288]{2,0,1:T(8,128)(2,1)S(1)}, u32[]{:S(2)}, u32[]{:S(2)}) async-start(bf16[180,8,288]{2,0,1:T(8,128)(2,1)} %select_bitcast_fusion), calls=%async_computation.5 | async-start | bytes 2260992 | tf_op jit(solution)/shard_map/all_to_all | solution.py:200
  305.7 1.0 copy-start.2
  306.7 21.8 %all-to-all-start.1 = ((bf16[2,8,288,180]{2,0,3,1:T(2,128)(2,1)}), bf16[2,8,288,180]{2,0,3,1:T(2,128)(2,1)S(1)}, u32[]{:S(2)}, u32[]{:S(2)}) async-start(bf16[2,8,288,180]{2,0,3,1:T(2,128)(2,1)} %fusion.16), calls=%async_computation.2 | async-start | bytes 4423680 | tf_op jit(solution)/shard_map/all_to_all | solution.py:199
  312.9 176.6 %reduce-scatter.7.cloned.1.call-start = ((), (), s32[]{:S(2)}) async-start(), calls=%async_computation.12 | async-start | bytes 9732096
  361.0 2.0 copy-start.5
  491.1 13.1 %all-to-all-start.5 = ((bf16[8,8,2304]{2,1,0:T(8,128)(2,1)}), bf16[8,8,2304]{2,1,0:T(8,128)(2,1)}, u32[]{:S(2)}, u32[]{:S(2)}) async-start(bf16[8,8,2304]{2,1,0:T(8,128)(2,1)} %copy.71), calls=%async_computation.6 | async-start | bytes 589824 | tf_op jit(solution)/shard_map/all_to_all | solution.py:243
  496.1 10.0 %copy-start.1 = (bf16[256,2304]{1,0:T(8,128)(2,1)S(1)}, bf16[256,2304]{1,0:T(8,128)(2,1)}, u32[]{:S(2)}) copy-start(bf16[256,2304]{1,0:T(8,128)(2,1)} %param.18) | copy-start | bytes 3538948
Sparse Core Ops, SparseCore 0:
  20.9 58.7 all-gather.4
  82.8 53.3 all-gather.8
  146.0 35.1 reduce-scatter.4
  195.6 97.8 all-gather.6
  361.2 128.2 reduce-scatter.6
where the time goes:
time: 514 us; the launch traced here: 513 us
  waiting for transfers between devices  353 us (69%)
  local copies, waits for them, and re-layouts  58.8 us (11%)
  matrix products  27.2 us (5%)
  starting transfers between devices  27.1 us (5%)
  other arithmetic  19.4 us (4%)
  between operations  14.7 us (3%)
  blocking collectives  12.7 us (2%)
    unnamed x6, waiting for transfers between devices  126 us
    all_gather x1, waiting for transfers between devices, shards(): lax.all_gather(value_block, 'seq', axis=0, tiled=True)  56.4 us
    all_gather x1, waiting for transfers between devices, shards(): lax.all_gather(key_block, 'seq', axis=0, tiled=True)  55.6 us
    all_to_all x1, waiting for transfers between devices, shards(): lax.all_to_all(gate_split, 'exp', split_axis=1, concat_axis=1, tiled=True)  52.2 us
    reduce_scatter x1, waiting for transfers between devices, shards(): lax.psum_scatter(jnp.dot(rows_in, w_out, preferred_element_type=jnp.float...  34.4 us
    unnamed x27, local copies, waits for them, and re-layouts  23.6 us
    all_to_all x1, blocking collectives, shards(): lax.all_to_all(outgoing, 'exp', split_axis=0, concat_axis=0, tiled=True)  12.7 us
    all_to_all x1, waiting for transfers between devices, shards(): lax.all_to_all(gate_sorted, 'exp', split_axis=1, concat_axis=1, tiled=True)  12.4 us
  transfers between devices with their start and end apart: 10, of which 8 were waited for; matrix products, arithmetic and copies ran while one was open for 10% of the time, Pallas kernels for 0%

commit v1 on v0

--- a/solution.py
+++ b/solution.py
@@ -140,7 +140,9 @@
         jnp.zeros((heads_here, block_rows, HEAD_DIM), jnp.float32),
     )
     pieces = (
-        lax.all_gather(key_block, "seq", axis=0, tiled=True),
+        jnp.concatenate(
+            lax.all_to_all(jnp.stack([key_block] * lax.axis_size("seq")), "seq", 0, 0), axis=0
+        ),
         lax.all_gather(value_block, "seq", axis=0, tiled=True),
     )
     key_rows = jnp.arange(pieces[0].shape[0], dtype=jnp.int32)

time: 514 us -> 475 us (0.924)
  waiting for transfers between devices: 353 us -> 299 us
  starting transfers between devices: 27.1 us -> 42.8 us
    all_gather x1 -> x0, waiting for transfers between devices: 55.6 us -> none  [shards(): lax.all_gather(key_block, 'seq', axis=0, tiled=True)]
    all_to_all x0 -> x1, starting transfers between devices: none -> 11.4 us  [shards(): lax.all_to_all(jnp.stack([key_block] * lax.axis_size('seq')), 'seq', 0, 0)]
    unnamed x6 -> x5, waiting for transfers between devices: 126 us -> 127 us
    unnamed x27 -> x29, local copies, waits for them, and re-layouts: 23.6 us -> 23.6 us
  transfers between devices with their start and end apart: 10 -> 10, of which waited for: 8 -> 7; matrix products, arithmetic and copies ran while one was open for 10% -> 11% of each run, Pallas kernels for 0% -> 0%
where the time goes in v1:
time: 475 us; the launch traced here: 474 us
  waiting for transfers between devices  299 us (63%)
  local copies, waits for them, and re-layouts  60.7 us (13%)
  starting transfers between devices  42.8 us (9%)
  matrix products  26.5 us (6%)
  other arithmetic  18 us (4%)
  between operations  14.7 us (3%)
  blocking collectives  12.5 us (3%)
    unnamed x5, waiting for transfers between devices  127 us
    all_gather x1, waiting for transfers between devices, shards(): lax.all_gather(value_block, 'seq', axis=0, tiled=True)  60.1 us
    all_to_all x1, waiting for transfers between devices, shards(): lax.all_to_all(gate_split, 'exp', split_axis=1, concat_axis=1, tiled=True)  52.1 us
    reduce_scatter x1, waiting for transfers between devices, shards(): lax.psum_scatter(jnp.dot(rows_in, w_out, preferred_element_type=jnp.float...  37 us
    unnamed x29, local copies, waits for them, and re-layouts  23.6 us
    all_to_all x1, blocking collectives, shards(): lax.all_to_all(outgoing, 'exp', split_axis=0, concat_axis=0, tiled=True)  12.5 us
    all_to_all x1, waiting for transfers between devices, shards(): lax.all_to_all(gate_sorted, 'exp', split_axis=1, concat_axis=1, tiled=True)  12.4 us
    all_to_all x1, starting transfers between devices, shards(): lax.all_to_all(jnp.stack([key_block] * lax.axis_size('seq')), 'seq', 0, 0)  11.4 us
  transfers between devices with their start and end apart: 10, of which 7 were waited for; matrix products, arithmetic and copies ran while one was open for 11% of the time, Pallas kernels for 0%

profile of v1, /device:TPU:8, one launch (start us, length us, event | category | flops | bytes accessed | tf_op | source)
XLA Modules:
  0.0 474.3 jit_solution(297042093473740062)
XLA Ops:
  9.3 5.9 %copy.62 = bf16[2304,3,256]{0,2,1:T(8,128)(2,1)} copy(bf16[2304,3,256]{2,0,1:T(8,128)(2,1)} %param.17) | data formatting | bytes 7077888 | tf_op args[2]
  15.2 3.2 fusion.28
  21.4 11.4 %all-to-all-start = ((bf16[32,128,4,64]{1,3,2,0:T(8,128)(2,1)}), bf16[32,128,4,64]{1,3,2,0:T(8,128)(2,1)S(1)}, u32[]{:S(2)}, u32[]{:S(2)}) async-start(bf16[32,128,4,64]{1,3,2,0:T(8,128)(2,1)} %stack.4), calls=%async_computation | async-start | bytes 4194304 | tf_op jit(solution)/shard_map/all_to_all | solution.py:144
  33.2 2.0 fusion.44
  35.9 60.1 %all-gather.6.cloned.1.call-done = bf16[4096,1,4,64]{0,3,2,1:T(8,128)(2,1)} async-done(((bf16[128,1,4,64]{0,3,2,1:T(8,128)(2,1)}), bf16[4096,1,4,64]{0,3,2,1:T(8,128)(2,1)}) %all-gather.6.cloned.1.call-update) | async-done | bytes 2097168 | tf_op jit(solution)/shard_map/all_gather | solution.py:146
  96.0 7.7 %conditional.1 = (f32[4,128]{1,0:T(4,128)S(1)}, f32[4,128,64]{1,2,0:T(8,128)S(1)}) conditional(s32[]{:T(128)} %convert_element_type.85, () %tuple.16, (pred[128,4096]{1,0:T(8,128)(4,1)}, bf16[32,128,4,64]{1,3,2,0:T(8,128)(2,1)S(1)}, bf16[128,4,64]{0,2,1:T(8,128)(2,1)S(1)}, bf16[4096,4,64]{0,2,1:T(8,128)(2,1)}) %tuple.47), branch_computations={%region_7.8_spmd, %region_8.11_spmd} | conditional | flops 564133376 | bytes 41627720 | solution.py:99
  96.1 2.9 fusion
  98.9 2.3 fusion.3
  101.3 2.5 fusion.2
  105.9 37.0 %reduce-scatter.5.cloned.1.call-done = bf16[16,2304]{1,0:T(8,128)(2,1)} async-done(((bf16[128,2304]{1,0:T(8,128)(2,1)}), bf16[16,2304]{1,0:T(8,128)(2,1)}) %reduce-scatter.5.cloned.1.call-update) | async-done | bytes 73744 | tf_op jit(solution)/shard_map/reduce_scatter | solution.py:165
  144.6 12.5 %all_to_all.35 = bf16[8,8,2304]{2,1,0:T(8,128)(2,1)} all-to-all(bf16[8,8,2304]{2,1,0:T(8,128)(2,1)S(1)} %fusion.14), channel_id=1, replica_groups=mesh['seq'=32,'exp'=8] {'exp'}, dimensions={0} | all-to-all | bytes 589824 | tf_op jit(solution)/shard_map/all_to_all | solution.py:223
  160.0 4.9 %all-to-all-start.4 = ((bf16[180,8,288]{2,0,1:T(8,128)(2,1)}), bf16[180,8,288]{2,0,1:T(8,128)(2,1)S(1)}, u32[]{:S(2)}, u32[]{:S(2)}) async-start(bf16[180,8,288]{2,0,1:T(8,128)(2,1)} %copy.70), calls=%async_computation.5 | async-start | bytes 2260992 | tf_op jit(solution)/shard_map/all_to_all | solution.py:196
  164.9 5.4 %reshape.266 = bf16[2,8,288,180]{2,1,0,3:T(8,128)(2,1)S(1)} reshape(bf16[1,2,2304,180]{2,1,3,0:T(2,128)(2,1)} %param.21) | data formatting | bytes 3317760 | tf_op jit(solution)/shard_map/reshape | solution.py:192
  170.3 3.1 copy.67
  173.4 8.9 %all-to-all-done.4 = bf16[180,8,288]{2,0,1:T(8,128)(2,1)S(1)} async-done(((bf16[180,8,288]{2,0,1:T(8,128)(2,1)}), bf16[180,8,288]{2,0,1:T(8,128)(2,1)S(1)}, u32[]{:S(2)}, u32[]{:S(2)}) %all-to-all-start.4) | async-done | bytes 829472 | tf_op jit(solution)/shard_map/all_to_all | solution.py:196
  182.3 4.6 all-to-all-start.1
  188.6 2.4 select_bitcast_fusion
  191.1 52.1 %all-to-all-done.1 = bf16[2,8,288,180]{2,0,3,1:T(2,128)(2,1)S(1)} async-done(((bf16[2,8,288,180]{2,0,3,1:T(2,128)(2,1)}), bf16[2,8,288,180]{2,0,3,1:T(2,128)(2,1)S(1)}, u32[]{:S(2)}, u32[]{:S(2)}) %all-to-all-start.1) | async-done | bytes 1658912 | tf_op jit(solution)/shard_map/all_to_all | solution.py:195
  243.1 6.3 %all-to-all-start.5 = ((bf16[180,8,288]{2,0,1:T(8,128)(2,1)}), bf16[180,8,288]{2,0,1:T(8,128)(2,1)S(1)}, u32[]{:S(2)}, u32[]{:S(2)}) async-start(bf16[180,8,288]{2,0,1:T(8,128)(2,1)} %select_bitcast_fusion), calls=%async_computation.6 | async-start | bytes 2260992 | tf_op jit(solution)/shard_map/all_to_all | solution.py:202
  249.5 6.3 %gather_fusion = bf16[8,2,288,180]{2,1,3,0:T(2,128)(2,1)} fusion(bf16[2,8,288,180]{2,0,3,1:T(2,128)(2,1)S(1)} %all-to-all-done.1, s32[1024]{0:T(1024)S(1)} %pad_clamp_fusion), kind=kCustom, calls=%fused_computation | custom fusion | bytes 3317792 | tf_op jit(solution)/shard_map/jit(_take)/gather | solution.py:198
  255.8 4.9 %fusion.19 = bf16[2,8,288,180]{2,0,3,1:T(2,128)(2,1)} fusion(bf16[8,2,288,180]{2,1,3,0:T(2,128)(2,1)} %gather_fusion, pred[8]{0:T(512)(128)(4,1)S(1)} %compare_and_fusion), kind=kLoop, calls=%fused_computation.26 | loop fusion | flops 829440 | bytes 3317768 | tf_op jit(solution)/shard_map/jit(_take)/select_n | solution.py:198
  260.8 2.1 all-to-all-done.5
  263.8 10.5 %all-to-all-start.2 = ((bf16[2,8,288,180]{2,0,3,1:T(2,128)(2,1)}), bf16[2,8,288,180]{2,0,3,1:T(2,128)(2,1)S(1)}, u32[]{:S(2)}, u32[]{:S(2)}) async-start(bf16[2,8,288,180]{2,0,3,1:T(2,128)(2,1)} %fusion.19), calls=%async_computation.3 | async-start | bytes 4423680 | tf_op jit(solution)/shard_map/all_to_all | solution.py:201
  277.6 12.4 %all-to-all-done.2 = bf16[2,8,288,180]{2,0,3,1:T(2,128)(2,1)S(1)} async-done(((bf16[2,8,288,180]{2,0,3,1:T(2,128)(2,1)}), bf16[2,8,288,180]{2,0,3,1:T(2,128)(2,1)S(1)}, u32[]{:S(2)}, u32[]{:S(2)}) %all-to-all-start.2) | async-done | bytes 1658912 | tf_op jit(solution)/shard_map/all_to_all | solution.py:201
  291.6 4.2 squeeze_reshape.6
  295.8 6.8 %fusion.16 = f32[2,2048,180]{1,2,0:T(8,128)S(1)} fusion(bf16[2,2304,180]{1,2,0:T(8,128)(2,1)} %squeeze_reshape.6, bf16[256,8,2304]{2,1,0:T(8,128)(2,1)} %all-gather.4.cloned.1.call-done), kind=kOutput, calls=%fused_computation.25 | convolution fusion | flops 3397386240 | bytes 14045184 | tf_op jit(solution)/shard_map/rd,cdf->crf/dot_general | solution.py:228
  304.0 2.2 copy.69
  306.2 7.8 %convert_bitcast_fusion = bf16[8,32,8,2304]{3,2,1,0:T(8,128)(2,1)} fusion(bf16[180,2304,1]{1,0,2:T(8,128)(2,1)} %reshape.265, bf16[256,8,180]{2,1,0:T(8,128)(2,1)} %bitcast.81), kind=kOutput, calls=%fused_computation.18 | convolution fusion | flops 1703411712 | bytes 11003904 | tf_op jit(solution)/shard_map/dot_general | solution.py:234
  314.0 8.5 %copy.85 = bf16[8,32,8,2304]{3,2,0,1:T(8,128)(2,1)} copy(bf16[8,32,8,2304]{3,2,1,0:T(8,128)(2,1)} %convert_bitcast_fusion) | data formatting | bytes 18874368
  324.7 126.5 %reduce-scatter.7.cloned.1.call-done = bf16[8,18432]{1,0:T(8,128)(2,1)} async-done(((bf16[256,18432]{1,0:T(8,128)(2,1)}), bf16[8,18432]{1,0:T(8,128)(2,1)}) %reduce-scatter.7.cloned.1.call-update) | async-done | bytes 294928
  452.8 4.8 %all-to-all-start.6 = ((bf16[8,8,2304]{2,1,0:T(8,128)(2,1)}), bf16[8,8,2304]{2,1,0:T(8,128)(2,1)}, u32[]{:S(2)}, u32[]{:S(2)}) async-start(bf16[8,8,2304]{2,1,0:T(8,128)(2,1)} %copy.73), calls=%async_computation.7 | async-start | bytes 589824 | tf_op jit(solution)/shard_map/all_to_all | solution.py:245
  459.6 6.3 %reshape.268 = bf16[1,2,2304,180]{2,1,3,0:T(2,128)(2,1)} reshape(bf16[2,8,288,180]{2,1,0,3:T(8,128)(2,1)} %copy.80) | data formatting | bytes 3317760
  (97 shorter events, 28.6 us)
Async XLA Ops:
  7.2 96.7 %copy-start = (bf16[256,2304]{1,0:T(8,128)(2,1)S(1)}, bf16[256,2304]{1,0:T(8,128)(2,1)}, u32[]{:S(2)}) copy-start(bf16[256,2304]{1,0:T(8,128)(2,1)} %param.18) | copy-start | bytes 3538948
  7.2 88.9 %all-gather.6.cloned.1.call-start = ((), (), s32[]{:S(2)}) async-start(), calls=%async_computation.11 | async-start | bytes 2162688 | tf_op jit(solution)/shard_map/all_gather | solution.py:146
  9.3 5.9 %copy-start.4 = (bf16[128,2304]{1,0:T(8,128)(2,1)S(1)}, bf16[128,2304]{1,0:T(8,128)(2,1)}, u32[]{:S(2)}) copy-start(bf16[128,2304]{1,0:T(8,128)(2,1)} %param.15) | copy-start | bytes 1769476
  15.2 3.9 copy-start.10
  21.4 11.6 %copy-start.9 = (s32[1,32]{1,0:T(1,128)S(1)}, s32[1,32]{1,0:T(1,128)}, u32[]{:S(2)}) copy-start(s32[1,32]{1,0:T(1,128)} %param.24) | copy-start | bytes 388
  21.4 74.7 %all-to-all-start = ((bf16[32,128,4,64]{1,3,2,0:T(8,128)(2,1)}), bf16[32,128,4,64]{1,3,2,0:T(8,128)(2,1)S(1)}, u32[]{:S(2)}, u32[]{:S(2)}) async-start(bf16[32,128,4,64]{1,3,2,0:T(8,128)(2,1)} %stack.4), calls=%async_computation | async-start | bytes 4194304 | tf_op jit(solution)/shard_map/all_to_all | solution.py:144
  32.8 110.1 %reduce-scatter.5.cloned.1.call-start = ((), (), s32[]{:S(2)}) async-start(), calls=%async_computation.9 | async-start | bytes 663552 | tf_op jit(solution)/shard_map/reduce_scatter | solution.py:165
  96.0 2.9 copy-start.2
  96.1 2.9 copy-start.12
  103.8 1.3 copy-start.8
  103.8 1.5 copy-start.7
  103.8 1.7 copy-start.13
  103.8 1.7 copy-start.11
  103.9 53.3 %copy-start.5 = (bf16[1,180,2304]{2,1,0:T(8,128)(2,1)S(1)}, bf16[1,180,2304]{2,1,0:T(8,128)(2,1)}, u32[]{:S(2)}) copy-start(bf16[1,180,2304]{2,1,0:T(8,128)(2,1)} %param.22) | copy-start | bytes 2488324
  105.1 190.8 %all-gather.4.cloned.1.call-start = ((), (), s32[]{:S(2)}) async-start(), calls=%async_computation.10 | async-start | bytes 9732096 | tf_op jit(solution)/shard_map/all_gather | solution.py:226
  160.0 22.3 %all-to-all-start.4 = ((bf16[180,8,288]{2,0,1:T(8,128)(2,1)}), bf16[180,8,288]{2,0,1:T(8,128)(2,1)S(1)}, u32[]{:S(2)}, u32[]{:S(2)}) async-start(bf16[180,8,288]{2,0,1:T(8,128)(2,1)} %copy.70), calls=%async_computation.5 | async-start | bytes 2260992 | tf_op jit(solution)/shard_map/all_to_all | solution.py:196
  182.3 60.9 %all-to-all-start.1 = ((bf16[2,8,288,180]{2,0,3,1:T(2,128)(2,1)}), bf16[2,8,288,180]{2,0,3,1:T(2,128)(2,1)S(1)}, u32[]{:S(2)}, u32[]{:S(2)}) async-start(bf16[2,8,288,180]{2,0,3,1:T(2,128)(2,1)} %copy.67), calls=%async_computation.2 | async-start | bytes 4423680 | tf_op jit(solution)/shard_map/all_to_all | solution.py:195
  243.1 19.7 %all-to-all-start.5 = ((bf16[180,8,288]{2,0,1:T(8,128)(2,1)}), bf16[180,8,288]{2,0,1:T(8,128)(2,1)S(1)}, u32[]{:S(2)}, u32[]{:S(2)}) async-start(bf16[180,8,288]{2,0,1:T(8,128)(2,1)} %select_bitcast_fusion), calls=%async_computation.6 | async-start | bytes 2260992 | tf_op jit(solution)/shard_map/all_to_all | solution.py:202
  262.8 1.0 copy-start.3
  263.8 26.2 %all-to-all-start.2 = ((bf16[2,8,288,180]{2,0,3,1:T(2,128)(2,1)}), bf16[2,8,288,180]{2,0,3,1:T(2,128)(2,1)S(1)}, u32[]{:S(2)}, u32[]{:S(2)}) async-start(bf16[2,8,288,180]{2,0,3,1:T(2,128)(2,1)} %fusion.19), calls=%async_computation.3 | async-start | bytes 4423680 | tf_op jit(solution)/shard_map/all_to_all | solution.py:201
  274.3 176.8 %reduce-scatter.7.cloned.1.call-start = ((), (), s32[]{:S(2)}) async-start(), calls=%async_computation.12 | async-start | bytes 9732096
  322.5 2.0 copy-start.6
  452.8 13.1 %all-to-all-start.6 = ((bf16[8,8,2304]{2,1,0:T(8,128)(2,1)}), bf16[8,8,2304]{2,1,0:T(8,128)(2,1)}, u32[]{:S(2)}, u32[]{:S(2)}) async-start(bf16[8,8,2304]{2,1,0:T(8,128)(2,1)} %copy.73), calls=%async_computation.7 | async-start | bytes 589824 | tf_op jit(solution)/shard_map/all_to_all | solution.py:245
  457.8 10.0 %copy-start.1 = (bf16[256,2304]{1,0:T(8,128)(2,1)S(1)}, bf16[256,2304]{1,0:T(8,128)(2,1)}, u32[]{:S(2)}) copy-start(bf16[256,2304]{1,0:T(8,128)(2,1)} %param.18) | copy-start | bytes 3538948
Sparse Core Ops, SparseCore 0:
  19.1 76.8 all-gather.5
  105.2 37.7 reduce-scatter.4
  157.3 97.7 all-gather.3
  322.6 128.4 reduce-scatter.6
